TPU v7x, 32 devices: a whole 2x2x4 slice. The times are simulated.
32 devices in a mesh: dp: 2 (over core), row: 4 (over y, x), col: 4 (over z).
Axes of the slice: x: 2, y: 2, z: 4, core: 2. Of those that a mesh axis runs over, the one named last changes fastest.
Arguments:
- hidden: bfloat16 [2048, 1024], P(('dp', 'row')), may hold values from -6 to 6
- segments: int32 [2, 1024], P('dp'), may hold values from 0 to 3, never falling along the last dimension, each value on 1 to 512 neighbouring positions
- cotangent: bfloat16 [2048, 1024], P(('dp', 'row')), may hold values from -6 to 6
- norm_gain: float32 [2, 1024], replicated, may hold values from 0.5 to 1.5
- zx_weight: bfloat16 [2, 1024, 4096], P(None, 'col', 'row'), may hold values from -0.1875 to 0.1875
- dt_weight: bfloat16 [2, 1024, 32], P(None, 'col', 'row'), may hold values from -0.1875 to 0.1875
- bc_weight: bfloat16 [2, 1024, 256], replicated, may hold values from -0.1875 to 0.1875
- conv_x: float32 [2, 4, 2048], P(None, None, ('row', 'col')), may hold values from -3 to 3
- conv_x_bias: float32 [2, 2048], P(None, ('row', 'col')), may hold values from -3 to 3
- conv_bc: float32 [2, 4, 256], replicated, may hold values from -3 to 3
- conv_bc_bias: float32 [2, 256], replicated, may hold values from -3 to 3
- dt_bias: float32 [2, 32], P(None, ('row', 'col')), may hold values from -6 to -2
- a_log: float32 [2, 32], P(None, ('row', 'col')), may hold values from -2 to 2.5
- skip_d: float32 [2, 32], P(None, ('row', 'col')), may hold values from 0.5 to 1.5
- gnorm_gain: float32 [2, 2048], P(None, ('row', 'col')), may hold values from 0.5 to 1.5
- out_weight: bfloat16 [2, 2048, 1024], P(None, ('row', 'col')), may hold values from -0.125 to 0.125
Outputs:
- hidden_out: bfloat16 [2048, 1024], P(('dp', 'row'))
- d_hidden: float32 [2048, 1024], P(('dp', 'row'))
- d_norm_gain: float32 [2, 1024], replicated
- d_zx_weight: float32 [2, 1024, 4096], P(None, 'col', 'row')
- d_dt_weight: float32 [2, 1024, 32], P(None, 'col', 'row')
- d_bc_weight: float32 [2, 1024, 256], replicated
- d_conv_x: float32 [2, 4, 2048], P(None, None, ('row', 'col'))
- d_conv_x_bias: float32 [2, 2048], P(None, ('row', 'col'))
- d_conv_bc: float32 [2, 4, 256], replicated
- d_conv_bc_bias: float32 [2, 256], replicated
- d_dt_bias: float32 [2, 32], P(None, ('row', 'col'))
- d_a_log: float32 [2, 32], P(None, ('row', 'col'))
- d_skip_d: float32 [2, 32], P(None, ('row', 'col'))
- d_gnorm_gain: float32 [2, 2048], P(None, ('row', 'col'))
- d_out_weight: float32 [2, 2048, 1024], P(None, ('row', 'col'))
Inputs may be any that keep to these rules, and one draw needn't show every extreme that they name: `segments`: within a sequence the document numbers never fall; each document is a run of 1 to 512 tokens, and in every sequence one document has exactly 512 tokens.
All inputs are finite; a program needn't handle non-finite values.
Results may differ from a plain program's by a relative error of at most 0.04.
Values may be sent and summed in bfloat16 or wider, within the bound.
No kernel may reach another device: no remote copies, remote signals or barrier semaphores. Data moves between devices by JAX's collectives and lax.ppermute only.
A program may use at most 128 MiB of HBM per device.

v0:
```python
from functools import partial
import jax
import jax.numpy as jnp
from jax import lax
from jax.sharding import PartitionSpec as P

HEADS = 32
HEAD_DIM = 64
BLOCK = 256
EPS = 1e-05
HIGHEST = lax.Precision.HIGHEST
CONTRACT_ROWS = (((0,), (0,)), ((), ()))
CONTRACT_COLS = (((1,), (1,)), ((), ()))


def shortened(array):

    def short(part):
        return part.astype(jnp.bfloat16) if part.dtype == jnp.float32 else part

    return jax.tree.map(short, array)


def conv_masks(seg_ids, taps):
    seg_masks = [jnp.ones(seg_ids.shape, jnp.float32)]
    for offset in range(1, taps):
        earlier = jnp.concatenate(
            [jnp.full((seg_ids.shape[0], offset), -1, jnp.int32), seg_ids[:, :-offset]], axis=1
        )
        seg_masks.append((earlier == seg_ids).astype(jnp.float32))
    return seg_masks


def causal_conv(values, kernel, conv_bias, seg_masks):
    running = conv_bias + kernel[0] * values
    for offset in range(1, kernel.shape[0]):
        padding = jnp.zeros((values.shape[0], offset, values.shape[2]), jnp.float32)
        shifted = jnp.concatenate([padding, values[:, :-offset]], axis=1)
        running = running + kernel[offset] * shifted * seg_masks[offset][:, :, None]
    return running


def mixer_piece(
    seg_ids,
    block,
    mixed_in,
    step_in,
    side_in,
    conv_x,
    conv_x_bias,
    conv_bc,
    conv_bc_bias,
    dt_bias,
    a_log,
    skip_d,
):
    seq_count, length = seg_ids.shape
    heads = step_in.shape[1]
    head_dim = mixed_in.shape[1] // (2 * heads)
    state = side_in.shape[1] // 2
    blocks = length // block
    seg_masks = conv_masks(seg_ids, conv_x.shape[0])
    halves = mixed_in.reshape(seq_count, length, heads, 2, head_dim)
    gate_in = halves[:, :, :, 0, :]
    values = halves[:, :, :, 1, :].reshape(seq_count, length, heads * head_dim)
    values = jax.nn.silu(causal_conv(values, conv_x, conv_x_bias, seg_masks))
    side = jax.nn.silu(
        causal_conv(side_in.reshape(seq_count, length, 2 * state), conv_bc, conv_bc_bias, seg_masks)
    )
    steps = jax.nn.softplus(step_in.reshape(seq_count, length, heads) + dt_bias)
    layout = (seq_count, blocks, block)
    inputs = side[:, :, :state].reshape(layout + (state,))
    readout = side[:, :, state:].reshape(layout + (state,))
    sources = values.reshape(layout + (heads, head_dim))
    steps_head = steps.reshape(layout + (heads,)).transpose(0, 1, 3, 2)
    decays = jnp.cumsum(steps_head * (-jnp.exp(a_log))[:, None], axis=3)
    seg_layout = seg_ids.reshape(layout)
    places = jnp.arange(block)
    causal = places[:, None] >= places[None, :]
    allowed = (seg_layout[:, :, :, None] == seg_layout[:, :, None, :]) & causal
    spans = decays[:, :, :, :, None] - decays[:, :, :, None, :]
    weights = jnp.exp(jnp.where(allowed[:, :, None], spans, -1e30))
    affinity = jnp.einsum("scqn,sckn->scqk", readout, inputs, precision=HIGHEST)
    scores = affinity[:, :, None] * weights * steps_head[:, :, :, None, :]
    result = jnp.einsum("schqk,sckhp->scqhp", scores, sources, precision=HIGHEST)
    last_seg = seg_layout[:, :, -1]
    same_last = (seg_layout == last_seg[:, :, None]).astype(jnp.float32)
    to_end = jnp.exp(decays[:, :, :, -1:] - decays) * same_last[:, :, None, :] * steps_head
    scaled = sources * to_end.transpose(0, 1, 3, 2)[..., None]
    states = jnp.einsum("sckn,sckhp->schnp", inputs, scaled, precision=HIGHEST)
    carried = states[:, 0]
    outputs = [jnp.zeros((seq_count, block, heads, head_dim), jnp.float32)]
    for index in range(1, blocks):
        keeper = (seg_layout[:, index] == last_seg[:, index - 1][:, None]).astype(jnp.float32)
        factor = jnp.exp(decays[:, index]) * keeper[:, None, :]
        earlier = jnp.einsum("sqn,shnp->sqhp", readout[:, index], carried, precision=HIGHEST)
        outputs.append(earlier * factor.transpose(0, 2, 1)[..., None])
        if index + 1 < blocks:
            linked = (last_seg[:, index] == last_seg[:, index - 1]).astype(jnp.float32)
            carry_decay = jnp.exp(decays[:, index, :, -1]) * linked[:, None]
            carried = states[:, index] + carry_decay[:, :, None, None] * carried
    result = result + jnp.stack(outputs, axis=1) + skip_d[:, None] * sources
    gated = result.reshape(seq_count, length, heads, head_dim) * jax.nn.silu(gate_in)
    return gated.reshape(seq_count * length, heads * head_dim)


def total_heads(terms):
    return jax.tree.map(lambda part: part.astype(jnp.float32), lax.psum(shortened(terms), "dp"))


def total_shared(terms):
    return lax.psum(terms, ("dp", "row", "col"))


def shards(
    hidden,
    segments,
    cotangent,
    norm_gain,
    zx_weight,
    dt_weight,
    bc_weight,
    conv_x,
    conv_x_bias,
    conv_bc,
    conv_bc_bias,
    dt_bias,
    a_log,
    skip_d,
    gnorm_gain,
    out_weight,
):
    col_count = lax.axis_size("col")
    row_count_axis = lax.axis_size("row")
    col_index = lax.axis_index("col")
    width = hidden.shape[1]
    col_width = width // col_count
    layers = zx_weight.shape[0]
    state_width = bc_weight.shape[2]
    inner_total = HEADS * HEAD_DIM
    rows_here = hidden.shape[0]
    resid = hidden.astype(jnp.float32)
    stored = []
    for layer_index in range(layers):
        scale = lax.rsqrt(jnp.mean(resid * resid, axis=1, keepdims=True) + EPS)
        normed = (resid * scale * norm_gain[layer_index]).astype(jnp.bfloat16)
        side = jnp.dot(normed, bc_weight[layer_index], preferred_element_type=jnp.float32).astype(
            jnp.bfloat16
        )
        normed_cols = lax.dynamic_slice_in_dim(normed, col_index * col_width, col_width, 1)
        gathered_cols, side_all = (
            lax.all_gather(normed_cols, "row", axis=0, tiled=True),
            lax.all_gather(side, "row", axis=0, tiled=True),
        )
        part_mixed = jnp.dot(
            gathered_cols, zx_weight[layer_index], preferred_element_type=jnp.float32
        )
        part_steps = jnp.dot(
            gathered_cols, dt_weight[layer_index], preferred_element_type=jnp.float32
        )
        mixed_sum, step_sum = (
            lax.psum_scatter(part_mixed, "col", scatter_dimension=1, tiled=True),
            lax.psum_scatter(part_steps, "col", scatter_dimension=1, tiled=True),
        )
        mixed_in = mixed_sum.astype(jnp.bfloat16)
        step_in = step_sum.astype(jnp.bfloat16)
        piece = partial(mixer_piece, segments, BLOCK)
        gated, pullback = jax.vjp(
            piece,
            mixed_in.astype(jnp.float32),
            step_in.astype(jnp.float32),
            side_all.astype(jnp.float32),
            conv_x[layer_index],
            conv_x_bias[layer_index],
            conv_bc[layer_index],
            conv_bc_bias[layer_index],
            dt_bias[layer_index],
            a_log[layer_index],
            skip_d[layer_index],
        )
        squares = lax.psum(jnp.sum(gated * gated, axis=1), ("row", "col"))
        inverse = lax.rsqrt(squares / inner_total + EPS)[:, None]
        normed_out = (gated * inverse * gnorm_gain[layer_index]).astype(jnp.bfloat16)

        def project(first_row, row_count, source=normed_out, weight=out_weight[layer_index]):
            return jnp.dot(source, weight, preferred_element_type=jnp.float32)

        kept_rows = normed_out.shape[0] // (row_count_axis * col_count)
        shared_rows = lax.psum_scatter(
            project(jnp.int32(0), lax.axis_size(("row", "col")) * kept_rows),
            ("row", "col"),
            scatter_dimension=0,
            tiled=True,
        )
        branch = lax.all_gather(shared_rows, "col", axis=0, tiled=True)
        stored.append((resid, scale, normed, gathered_cols, gated, inverse, normed_out, pullback))
        resid = resid + branch
    result_out = resid.astype(jnp.bfloat16)
    grad = cotangent.astype(jnp.float32)
    heads_terms = [None] * layers
    shared_terms = [None] * layers
    for layer_index in reversed(range(layers)):
        resid_in, scale, normed, gathered_cols, gated, inverse, normed_out, pullback = stored[
            layer_index
        ]
        grad_low = grad.astype(jnp.bfloat16)
        grad_full = lax.all_gather(grad_low, "row", axis=0, tiled=True)
        grad_out_w = lax.dot_general(
            normed_out, grad_full, CONTRACT_ROWS, preferred_element_type=jnp.float32
        )
        grad_normed_out = lax.dot_general(
            grad_full, out_weight[layer_index], CONTRACT_COLS, preferred_element_type=jnp.float32
        )
        grad_gnorm = jnp.sum(grad_normed_out * gated * inverse, axis=0)
        weighted = gnorm_gain[layer_index] * grad_normed_out
        inner_dot = lax.psum(jnp.sum(gated * weighted, axis=1), ("row", "col"))
        grad_gated = inverse * weighted - gated * inverse**3 * (inner_dot / inner_total)[:, None]
        (
            g_mixed,
            g_steps,
            g_side,
            g_conv_x,
            g_conv_x_bias,
            g_conv_bc,
            g_conv_bc_bias,
            g_dt_bias,
            g_a_log,
            g_skip,
        ) = pullback(grad_gated)
        mixed_rows, steps_rows = (
            lax.all_gather(g_mixed.astype(jnp.bfloat16), "col", axis=1, tiled=True),
            lax.all_gather(g_steps.astype(jnp.bfloat16), "col", axis=1, tiled=True),
        )
        grad_zx_w = lax.dot_general(
            gathered_cols, mixed_rows, CONTRACT_ROWS, preferred_element_type=jnp.float32
        )
        grad_dt_w = lax.dot_general(
            gathered_cols, steps_rows, CONTRACT_ROWS, preferred_element_type=jnp.float32
        )

        def back_rows(
            first_row,
            row_count,
            mixed_src=mixed_rows,
            steps_src=steps_rows,
            side_src=g_side,
            w_mixed=zx_weight[layer_index],
            w_steps=dt_weight[layer_index],
        ):
            main_part = lax.dot_general(
                mixed_src, w_mixed, CONTRACT_COLS, preferred_element_type=jnp.float32
            )
            main_part = main_part + lax.dot_general(
                steps_src, w_steps, CONTRACT_COLS, preferred_element_type=jnp.float32
            )
            return jnp.concatenate([main_part, side_src], axis=1)

        summed = lax.psum_scatter(
            back_rows(
                jnp.int32(0), lax.axis_size("row") * (mixed_rows.shape[0] // row_count_axis)
            ).astype(jnp.bfloat16),
            "row",
            scatter_dimension=0,
            tiled=True,
        ).astype(jnp.float32)
        all_cols = lax.all_gather(summed.astype(jnp.bfloat16), "col", axis=1, tiled=True).astype(
            summed.dtype
        )
        all_cols = all_cols.reshape(rows_here, col_count, col_width + state_width)
        grad_normed = all_cols[:, :, :col_width].reshape(rows_here, width)
        grad_side = jnp.sum(all_cols[:, :, col_width:], axis=1).astype(jnp.bfloat16)
        grad_normed = grad_normed + lax.dot_general(
            grad_side, bc_weight[layer_index], CONTRACT_COLS, preferred_element_type=jnp.float32
        )
        normed_local = lax.dynamic_slice_in_dim(normed, col_index * col_width, col_width, 1)
        bc_piece = lax.dot_general(
            normed_local, grad_side, CONTRACT_ROWS, preferred_element_type=jnp.float32
        )
        grad_bc_w = lax.dynamic_update_slice_in_dim(
            jnp.zeros((width, state_width), jnp.float32), bc_piece, col_index * col_width, 0
        )
        gain_terms = lax.dynamic_slice_in_dim(
            grad_normed * resid_in * scale, col_index * col_width, col_width, 1
        )
        grad_gain = lax.dynamic_update_slice_in_dim(
            jnp.zeros((width,), jnp.float32), jnp.sum(gain_terms, axis=0), col_index * col_width, 0
        )
        gain_dot = jnp.sum(resid_in * norm_gain[layer_index] * grad_normed, axis=1, keepdims=True)
        grad = (
            grad
            + scale * norm_gain[layer_index] * grad_normed
            - resid_in * scale**3 * gain_dot / width
        )
        head_tuple = (
            grad_zx_w,
            grad_dt_w,
            g_conv_x,
            g_conv_x_bias,
            g_dt_bias,
            g_a_log,
            g_skip,
            grad_gnorm,
            grad_out_w,
        )
        shared_tuple = (grad_gain, grad_bc_w, g_conv_bc, g_conv_bc_bias)
        heads_terms[layer_index] = head_tuple
        shared_terms[layer_index] = shared_tuple
    heads_stack = tuple(
        (jnp.stack([heads_terms[index][member] for index in range(layers)]) for member in range(9))
    )
    shared_stack = tuple(
        (jnp.stack([shared_terms[index][member] for index in range(layers)]) for member in range(4))
    )
    heads_stack = total_heads(heads_stack)
    shared_stack = total_shared(shared_stack)
    return (
        result_out,
        grad,
        shared_stack[0],
        heads_stack[0],
        heads_stack[1],
        shared_stack[1],
        heads_stack[2],
        heads_stack[3],
        shared_stack[2],
        shared_stack[3],
        heads_stack[4],
        heads_stack[5],
        heads_stack[6],
        heads_stack[7],
        heads_stack[8],
    )


def solution(mesh):
    placed = (
        P(("dp", "row"), None),
        P("dp", None),
        P(("dp", "row"), None),
        P(),
        P(None, "col", "row"),
        P(None, "col", "row"),
        P(),
        P(None, None, ("row", "col")),
        P(None, ("row", "col")),
        P(),
        P(),
        P(None, ("row", "col")),
        P(None, ("row", "col")),
        P(None, ("row", "col")),
        P(None, ("row", "col")),
        P(None, ("row", "col"), None),
    )
    return jax.shard_map(
        shards,
        mesh=mesh,
        in_specs=placed,
        out_specs=(
            P(("dp", "row"), None),
            P(("dp", "row"), None),
            P(),
            P(None, "col", "row"),
            P(None, "col", "row"),
            P(),
            P(None, None, ("row", "col")),
            P(None, ("row", "col")),
            P(),
            P(),
            P(None, ("row", "col")),
            P(None, ("row", "col")),
            P(None, ("row", "col")),
            P(None, ("row", "col")),
            P(None, ("row", "col"), None),
        ),
        check_vma=False,
    )
```

profile of v0, /device:TPU:0, one launch (start us, length us, event | category | flops | bytes accessed | tf_op | source)
XLA Modules:
  0.0 1166.4 jit_solution(9310738073706395560)
XLA Ops:
  12.0 11.5 all_gather.42
  23.6 2.7 fusion.148
  28.4 20.9 %all-reduce.74 = bf16[1024,8]{0,1:T(8,128)(2,1)S(1)} all-reduce(f32[1024,8]{0,1:T(8,128)S(1)} %fusion.316), channel_id=5, replica_groups=mesh['dp'=2,'row'=4,'col'=4] {'col'}, use_global_device_ids=true, to_apply=%region_2.0.clone | all-reduce | flops 8192 | bytes 49152
  50.6 2.4 reduce-window.26
  61.7 9.9 all_gather.43
  78.2 2.1 fusion.109
  82.4 22.0 %reduce-scatter.7.cloned.1.call-done = f32[1024,256]{1,0:T(8,128)} async-done(((f32[1024,1024]{1,0:T(8,128)}), f32[1024,256]{1,0:T(8,128)}) %reduce-scatter.7.cloned.1.call-update) | async-done | bytes 1048592 | tf_op jit(solution)/shard_map/reduce_scatter | solution.py:162
  104.3 2.3 convert_convert_fusion.1
  106.6 2.5 copy.258
  115.8 2.3 squeeze.43
  120.1 3.7 multiply_reduce_fusion.29
  123.8 41.3 %psum.119 = f32[1024]{0:T(1024)S(1)} all-reduce(f32[1024]{0:T(1024)S(1)} %bitcast.1228), channel_id=1, replica_groups=mesh['dp'=2,'row'=4,'col'=4] {'row','col'}, use_global_device_ids=true, to_apply=%region_6.8 | all-reduce | flops 1024 | bytes 8192 | tf_op jit(solution)/shard_map/psum | solution.py:181
  167.1 2.7 fusion.186
  169.9 93.9 %reduce-scatter.9.cloned.1.call-done = f32[64,1024]{1,0:T(8,128)} async-done(((f32[1024,1024]{1,0:T(8,128)}), f32[64,1024]{1,0:T(8,128)}) %reduce-scatter.9.cloned.1.call-update) | async-done | bytes 262160 | tf_op jit(solution)/shard_map/reduce_scatter | solution.py:189
  263.9 28.0 %all-gather.11.cloned.1.call-done = f32[256,1024]{1,0:T(8,128)} async-done(((f32[64,1024]{1,0:T(8,128)}), f32[256,1024]{1,0:T(8,128)}) %all-gather.11.cloned.1.call-update) | async-done | bytes 1048592 | tf_op jit(solution)/shard_map/all_gather | solution.py:195
  294.9 10.5 all_gather.45
  305.4 3.9 fusion.142
  312.0 19.0 %all-reduce.75 = bf16[1024,8]{0,1:T(8,128)(2,1)S(1)} all-reduce(f32[1024,8]{0,1:T(8,128)S(1)} %fusion.313), channel_id=8, replica_groups=mesh['dp'=2,'row'=4,'col'=4] {'col'}, use_global_device_ids=true, to_apply=%region_10.12.clone | all-reduce | flops 8192 | bytes 49152
  331.3 2.4 reduce-window.30
  335.1 13.8 %all_gather.46 = bf16[1024,256]{1,0:T(8,128)(2,1)S(1)} all-gather(bf16[256,256]{1,0:T(8,128)(2,1)S(1)} %convolution_convert_fusion.4), channel_id=1, replica_groups=mesh['dp'=2,'row'=4,'col'=4] {'row'}, dimensions={0}, use_global_device_ids=true | all-gather | bytes 655360 | tf_op jit(solution)/shard_map/all_gather | solution.py:153
  349.1 2.1 fusion.96
  353.0 3.1 fusion.386
  356.1 30.0 %reduce-scatter.11.cloned.1.call-done = f32[1024,256]{1,0:T(8,128)} async-done(((f32[1024,1024]{1,0:T(8,128)}), f32[1024,256]{1,0:T(8,128)}) %reduce-scatter.11.cloned.1.call-update) | async-done | bytes 1048592 | tf_op jit(solution)/shard_map/reduce_scatter | solution.py:162
  386.1 2.3 convert_convert_fusion
  388.4 2.6 copy.270
  407.9 3.6 multiply_reduce_fusion.28
  414.1 42.0 %psum.120 = f32[1024]{0:T(1024)} all-reduce(f32[1024]{0:T(1024)} %bitcast.1227), channel_id=1, replica_groups=mesh['dp'=2,'row'=4,'col'=4] {'row','col'}, use_global_device_ids=true, to_apply=%region_14.16 | all-reduce | flops 1024 | bytes 8192 | tf_op jit(solution)/shard_map/psum | solution.py:181
  457.4 4.5 multiply_reduce_fusion.14
  461.9 37.6 %psum.121 = f32[1024]{0:T(1024)} all-reduce(f32[1024]{0:T(1024)} %get-tuple-element.34), channel_id=1, replica_groups=mesh['dp'=2,'row'=4,'col'=4] {'row','col'}, use_global_device_ids=true, to_apply=%region_17.19 | all-reduce | flops 1024 | bytes 8192 | tf_op jit(solution)/shard_map/psum | solution.py:216
  500.2 3.2 fusion.124
  506.9 5.9 fusion.31
  518.7 2.5 convolution_bitcast_fusion.4
  529.0 3.7 fusion.36
  555.5 11.3 reduce-window.34
  579.2 14.0 %all-gather = bf16[1,1024,8]{1,0,2:T(2,128)(2,1)} all-gather(bf16[1,1024,2]{1,0,2:T(2,128)(2,1)S(1)} %copy.297), channel_id=2, replica_groups=mesh['dp'=2,'row'=4,'col'=4] {'col'}, dimensions={2}, use_global_device_ids=true | all-gather | bytes 20480 | tf_op jit(solution)/shard_map/all_gather | solution.py:232
  597.2 2.3 fusion.34
  604.8 2.3 fusion.140
  609.1 2.7 fusion.182
  611.9 22.6 %reduce-scatter.15.cloned.1.call-done = bf16[256,512]{1,0:T(8,128)(2,1)} async-done(((bf16[1024,512]{1,0:T(8,128)(2,1)}), bf16[256,512]{1,0:T(8,128)(2,1)}) %reduce-scatter.15.cloned.1.call-update) | async-done | bytes 262160 | tf_op jit(solution)/shard_map/reduce_scatter | solution.py:258
  634.6 115.4 %reduce-scatter.13.cloned.1.call-done = f32[64,1024]{1,0:T(8,128)} async-done(((f32[1024,1024]{1,0:T(8,128)}), f32[64,1024]{1,0:T(8,128)}) %reduce-scatter.13.cloned.1.call-update) | async-done | bytes 262160 | tf_op jit(solution)/shard_map/reduce_scatter | solution.py:189
  750.1 3.7 reshape.2426
  753.8 2.4 slice_reduce_fusion.1
  758.4 18.0 %all-gather.13.cloned.1.call-done = f32[256,1024]{1,0:T(8,128)} async-done(((f32[64,1024]{1,0:T(8,128)}), f32[256,1024]{1,0:T(8,128)}) %all-gather.13.cloned.1.call-update) | async-done | bytes 1048592 | tf_op jit(solution)/shard_map/all_gather | solution.py:195
  776.4 3.3 fusion.369
  783.6 30.7 %all-gather.21.cloned.1.call-done = bf16[1024,1024]{1,0:T(8,128)(2,1)} async-done(((bf16[256,1024]{1,0:T(8,128)(2,1)}), bf16[1024,1024]{1,0:T(8,128)(2,1)}) %all-gather.21.cloned.1.call-update) | async-done | bytes 2097168 | tf_op jit(solution)/shard_map/all_gather | solution.py:207
  814.3 4.4 multiply_reduce_fusion.15
  818.7 40.9 %psum.122 = f32[1024]{0:T(1024)S(1)} all-reduce(f32[1024]{0:T(1024)S(1)} %get-tuple-element.32), channel_id=1, replica_groups=mesh['dp'=2,'row'=4,'col'=4] {'row','col'}, use_global_device_ids=true, to_apply=%region_35.37 | all-reduce | flops 1024 | bytes 8192 | tf_op jit(solution)/shard_map/psum | solution.py:216
  859.7 3.2 fusion.125
  866.4 5.5 fusion.33
  880.9 3.7 fusion.45
  907.3 11.3 reduce-window.36
  930.9 14.0 %all-gather.1 = bf16[1,1024,8]{1,0,2:T(2,128)(2,1)} all-gather(bf16[1,1024,2]{1,0,2:T(2,128)(2,1)S(1)} %copy.319), channel_id=3, replica_groups=mesh['dp'=2,'row'=4,'col'=4] {'col'}, dimensions={2}, use_global_device_ids=true | all-gather | bytes 20480 | tf_op jit(solution)/shard_map/all_gather | solution.py:232
  948.5 2.3 fusion.35
  955.8 2.4 fusion.146
  962.6 2.2 fusion.55
  966.7 18.4 %reduce-scatter.17.cloned.1.call-done = bf16[256,512]{1,0:T(8,128)(2,1)} async-done(((bf16[1024,512]{1,0:T(8,128)(2,1)}), bf16[256,512]{1,0:T(8,128)(2,1)}) %reduce-scatter.17.cloned.1.call-update) | async-done | bytes 262160 | tf_op jit(solution)/shard_map/reduce_scatter | solution.py:258
  995.0 3.6 all-reduce.77
  1002.7 10.6 all-gather.25.cloned.1.call-done
  1013.3 3.7 reshape.2428
  1017.0 2.2 slice_reduce_fusion
  1022.6 2.8 convert_element_type.209
  1028.6 40.7 %all-reduce.76 = (f32[2,1024]{1,0:T(2,128)}, f32[2,4,256]{2,1,0:T(4,128)}, f32[2,256]{1,0:T(2,128)}) all-reduce(f32[2,1024]{1,0:T(2,128)S(1)} %pad_maximum_fusion.5, f32[2,4,256]{2,1,0:T(4,128)S(1)} %pad_maximum_fusion.7, f32[2,256]{1,0:T(2,128)S(1)} %pad_maximum_fusion.9), channel_id=1, replica_groups=mesh['dp'=2,'row'=4,'col'=4] {'dp','row','col'}, use_global_device_ids=true, to_apply=%region_54.56 | all-reduce | flops 4608 | bytes 36864 | tf_op jit(solution)/shard_map/psum | solution.py:112
  1070.7 85.3 %all-reduce.82.cloned.1.call-done = f32[2,1024,256]{2,1,0:T(8,128)} async-done(((f32[2,1024,256]{2,1,0:T(8,128)}), f32[2,1024,256]{2,1,0:T(8,128)}) %all-reduce.82.cloned.1.call-update) | async-done | bytes 2097168 | tf_op jit(solution)/shard_map/psum | solution.py:112
  1156.0 3.0 copy.438
  (787 shorter events, 214.3 us)
Async XLA Ops:
  8.0 96.3 %reduce-scatter.7.cloned.1.call-start = ((), (), s32[]{:S(2)}) async-start(), calls=%async_computation.6 | async-start | bytes 5242880 | tf_op jit(solution)/shard_map/reduce_scatter | solution.py:162
  8.9 285.1 %copy-start.111 = (f32[1,1024]{1,0:T(1,128)}, f32[1,1024]{1,0:T(1,128)S(1)}, u32[]{:S(2)}) copy-start(f32[1,1024]{1,0:T(1,128)S(1)} %get-tuple-element.187) | copy-start | bytes 12292
  12.0 49.4 %copy-start.54 = (bf16[256,1024]{1,0:T(8,128)(2,1)}, bf16[256,1024]{1,0:T(8,128)(2,1)S(1)}, u32[]{:S(2)}) copy-start(bf16[256,1024]{1,0:T(8,128)(2,1)S(1)} %fusion.68) | copy-start | bytes 1572868
  26.3 27.8 %copy-start.100 = (s32[1,1024]{1,0:T(1,128)S(1)}, s32[1,1024]{1,0:T(1,128)}, u32[]{:S(2)}) copy-start(s32[1,1024]{1,0:T(1,128)} %param.18) | copy-start | bytes 12292
  26.3 32.1 %copy-start.218 = (f32[2,128]{1,0:T(2,128)S(1)}, f32[2,128]{1,0:T(2,128)}, u32[]{:S(2)}) copy-start(f32[2,128]{1,0:T(2,128)} %param.31) | copy-start | bytes 3076
  26.3 35.1 %copy-start.68 = (bf16[2,1024,256]{2,1,0:T(8,128)(2,1)S(1)}, bf16[2,1024,256]{2,1,0:T(8,128)(2,1)}, u32[]{:S(2)}) copy-start(bf16[2,1024,256]{2,1,0:T(8,128)(2,1)} %param.23) | copy-start | bytes 3145732
  26.3 45.6 %copy-start.220 = (f32[2,128]{1,0:T(2,128)S(1)}, f32[2,128]{1,0:T(2,128)}, u32[]{:S(2)}) copy-start(f32[2,128]{1,0:T(2,128)} %param.25) | copy-start | bytes 3076
  26.3 46.1 %copy-start.221 = (f32[2,2]{1,0:T(2,128)S(1)}, f32[2,2]{1,0:T(2,128)}, u32[]{:S(2)}) copy-start(f32[2,2]{1,0:T(2,128)} %param.30) | copy-start | bytes 52
  26.4 46.7 %copy-start.214 = (f32[2,256]{1,0:T(2,128)S(1)}, f32[2,256]{1,0:T(2,128)}, u32[]{:S(2)}) copy-start(f32[2,256]{1,0:T(2,128)} %param.27) | copy-start | bytes 6148
  26.4 47.2 %copy-start.201 = (f32[2,4,128]{2,1,0:T(4,128)S(1)}, f32[2,4,128]{2,1,0:T(4,128)}, u32[]{:S(2)}) copy-start(f32[2,4,128]{2,1,0:T(4,128)} %param.24) | copy-start | bytes 12292
  26.4 49.9 %copy-start.166 = (f32[2,4,256]{2,1,0:T(4,128)S(1)}, f32[2,4,256]{2,1,0:T(4,128)}, u32[]{:S(2)}) copy-start(f32[2,4,256]{2,1,0:T(4,128)} %param.26) | copy-start | bytes 24580
  26.4 237.4 %reduce-scatter.9.cloned.1.call-start = ((), (), s32[]{:S(2)}) async-start(), calls=%async_computation.7 | async-start | bytes 4456448 | tf_op jit(solution)/shard_map/reduce_scatter | solution.py:189
  50.5 69.5 %copy-start.95 = (f32[1,1024,2]{1,2,0:T(2,128)}, f32[1,1024,2]{1,2,0:T(2,128)S(1)}, u32[]{:S(2)}) copy-start(f32[1,1024,2]{1,2,0:T(2,128)S(1)} %compare_select_fusion.5) | copy-start | bytes 24580
  71.8 47.0 %copy-start.159 = (f32[2]{0:T(128)}, f32[2]{0:T(128)S(1)}, u32[]{:S(2)}) copy-start(f32[2]{0:T(128)S(1)} %get-tuple-element.56) | copy-start | bytes 28
  71.8 47.0 %copy-start.184 = (f32[2]{0:T(128)}, f32[2]{0:T(128)S(1)}, u32[]{:S(2)}) copy-start(f32[2]{0:T(128)S(1)} %get-tuple-element.55) | copy-start | bytes 28
  74.2 37.1 %copy-start.167 = (f32[128]{0:T(128)}, f32[128]{0:T(128)S(1)}, u32[]{:S(2)}) copy-start(f32[128]{0:T(128)S(1)} %get-tuple-element.201) | copy-start | bytes 1540
  74.2 37.1 %copy-start.169 = (f32[128]{0:T(128)}, f32[128]{0:T(128)S(1)}, u32[]{:S(2)}) copy-start(f32[128]{0:T(128)S(1)} %get-tuple-element.198) | copy-start | bytes 1540
  74.2 37.1 %copy-start.171 = (f32[128]{0:T(128)}, f32[128]{0:T(128)S(1)}, u32[]{:S(2)}) copy-start(f32[128]{0:T(128)S(1)} %get-tuple-element.199) | copy-start | bytes 1540
  74.2 37.1 %copy-start.173 = (f32[128]{0:T(128)}, f32[128]{0:T(128)S(1)}, u32[]{:S(2)}) copy-start(f32[128]{0:T(128)S(1)} %get-tuple-element.200) | copy-start | bytes 1540
  76.2 276.1 %copy-start.99 = (f32[4,256]{1,0:T(4,128)}, f32[4,256]{1,0:T(4,128)S(1)}, u32[]{:S(2)}) copy-start(f32[4,256]{1,0:T(4,128)S(1)} %compare_convert_fusion.6) | copy-start | bytes 12292
  76.3 43.6 %copy-start.122 = (f32[256,2]{0,1:T(2,128)}, f32[256,2]{0,1:T(2,128)S(1)}, u32[]{:S(2)}) copy-start(f32[256,2]{0,1:T(2,128)S(1)} %get-tuple-element.189) | copy-start | bytes 6148
  76.3 43.7 %copy-start.124 = (f32[256,2]{0,1:T(2,128)}, f32[256,2]{0,1:T(2,128)S(1)}, u32[]{:S(2)}) copy-start(f32[256,2]{0,1:T(2,128)S(1)} %get-tuple-element.190) | copy-start | bytes 6148
  76.3 43.7 %copy-start.126 = (f32[256,2]{0,1:T(2,128)}, f32[256,2]{0,1:T(2,128)S(1)}, u32[]{:S(2)}) copy-start(f32[256,2]{0,1:T(2,128)S(1)} %get-tuple-element.191) | copy-start | bytes 6148
  77.0 316.1 %copy-start.83 = (f32[1,1024]{1,0:T(1,128)}, f32[1,1024]{1,0:T(1,128)S(1)}, u32[]{:S(2)}) copy-start(f32[1,1024]{1,0:T(1,128)S(1)} %get-tuple-element.207) | copy-start | bytes 12292
  77.0 316.1 %copy-start.86 = (f32[1,1024]{1,0:T(1,128)}, f32[1,1024]{1,0:T(1,128)S(1)}, u32[]{:S(2)}) copy-start(f32[1,1024]{1,0:T(1,128)S(1)} %get-tuple-element.208) | copy-start | bytes 12292
  77.0 316.1 %copy-start.89 = (f32[1,1024]{1,0:T(1,128)}, f32[1,1024]{1,0:T(1,128)S(1)}, u32[]{:S(2)}) copy-start(f32[1,1024]{1,0:T(1,128)S(1)} %get-tuple-element.209) | copy-start | bytes 12292
  77.1 41.0 %copy-start.105 = (f32[4,256,2]{1,2,0:T(2,128)}, f32[4,256,2]{1,2,0:T(2,128)S(1)}, u32[]{:S(2)}) copy-start(f32[4,256,2]{1,2,0:T(2,128)S(1)} %multiply_bitcast_fusion.7) | copy-start | bytes 24580
  80.4 37.7 %copy-start.4 = (f32[1,1024,128]{2,1,0:T(8,128)}, f32[1,1024,128]{2,1,0:T(8,128)S(1)}, u32[]{:S(2)}) copy-start(f32[1,1024,128]{2,1,0:T(8,128)S(1)} %get-tuple-element.150) | copy-start | bytes 1572868
  80.4 39.2 %copy-start.13 = (f32[1,1024,128]{2,1,0:T(8,128)}, f32[1,1024,128]{2,1,0:T(8,128)S(1)}, u32[]{:S(2)}) copy-start(f32[1,1024,128]{2,1,0:T(8,128)S(1)} %get-tuple-element.151) | copy-start | bytes 1572868
  120.1 45.7 %copy-start.217 = (f32[2,64]{1,0:T(2,128)S(1)}, f32[2,64]{1,0:T(2,128)}, u32[]{:S(2)}) copy-start(f32[2,64]{1,0:T(2,128)} %mul.2202) | copy-start | bytes 1540
  120.1 47.0 %copy-start.79 = (bf16[2,128,1024]{2,1,0:T(8,128)(2,1)S(1)}, bf16[2,128,1024]{2,1,0:T(8,128)(2,1)}, u32[]{:S(2)}) copy-start(bf16[2,128,1024]{2,1,0:T(8,128)(2,1)} %param.32) | copy-start | bytes 1572868
  169.9 122.0 %copy-start.2 = (bf16[256,1024]{1,0:T(8,128)(2,1)S(1)}, bf16[256,1024]{1,0:T(8,128)(2,1)}, u32[]{:S(2)}) copy-start(bf16[256,1024]{1,0:T(8,128)(2,1)} %param.17) | copy-start | bytes 1572868
  169.9 122.0 %all-gather.11.cloned.1.call-start = ((), (), s32[]{:S(2)}) async-start(), calls=%async_computation.8 | async-start | bytes 1310720 | tf_op jit(solution)/shard_map/all_gather | solution.py:195
  263.8 122.2 %reduce-scatter.11.cloned.1.call-start = ((), (), s32[]{:S(2)}) async-start(), calls=%async_computation.9 | async-start | bytes 5242880 | tf_op jit(solution)/shard_map/reduce_scatter | solution.py:162
  309.4 25.1 %copy-start.134 = (f32[1,1,256]{2,1,0:T(1,128)S(1)}, f32[1,1,256]{2,1,0:T(1,128)}, u32[]{:S(2)}) copy-start(f32[1,1,256]{2,1,0:T(1,128)} %copy-done.133) | copy-start | bytes 3076
  309.4 25.1 %copy-start.136 = (f32[1,1,256]{2,1,0:T(1,128)S(1)}, f32[1,1,256]{2,1,0:T(1,128)}, u32[]{:S(2)}) copy-start(f32[1,1,256]{2,1,0:T(1,128)} %copy-done.135) | copy-start | bytes 3076
  309.4 147.9 %all-gather.15.cloned.1.call-start = ((), (), s32[]{:S(2)}) async-start(), calls=%async_computation.12 | async-start | bytes 2621440 | tf_op jit(solution)/shard_map/all_gather | solution.py:207
  310.0 39.0 %copy-start.149 = (f32[1,1,256]{2,1,0:T(1,128)S(1)}, f32[1,1,256]{2,1,0:T(1,128)}, u32[]{:S(2)}) copy-start(f32[1,1,256]{2,1,0:T(1,128)} %get-tuple-element.185) | copy-start | bytes 3076
  310.0 39.0 %copy-start.151 = (f32[1,1,256]{2,1,0:T(1,128)S(1)}, f32[1,1,256]{2,1,0:T(1,128)}, u32[]{:S(2)}) copy-start(f32[1,1,256]{2,1,0:T(1,128)} %get-tuple-element.186) | copy-start | bytes 3076
  310.0 39.0 %copy-start.153 = (f32[1,1,256]{2,1,0:T(1,128)S(1)}, f32[1,1,256]{2,1,0:T(1,128)}, u32[]{:S(2)}) copy-start(f32[1,1,256]{2,1,0:T(1,128)} %get-tuple-element.180) | copy-start | bytes 3076
  310.0 39.0 %copy-start.157 = (f32[1,1,256]{2,1,0:T(1,128)S(1)}, f32[1,1,256]{2,1,0:T(1,128)}, u32[]{:S(2)}) copy-start(f32[1,1,256]{2,1,0:T(1,128)} %get-tuple-element.179) | copy-start | bytes 3076
  310.1 39.0 %copy-start.193 = (f32[1,256]{1,0:T(1,128)S(1)}, f32[1,256]{1,0:T(1,128)}, u32[]{:S(2)}) copy-start(f32[1,256]{1,0:T(1,128)} %get-tuple-element.210) | copy-start | bytes 3076
  310.1 294.4 %all-gather.17.cloned.1.call-start = ((), (), s32[]{:S(2)}) async-start(), calls=%async_computation.13 | async-start | bytes 2621440 | tf_op jit(solution)/shard_map/all_gather | solution.py:231
  334.5 68.6 %copy-start.161 = (f32[2]{0:T(128)}, f32[2]{0:T(128)S(1)}, u32[]{:S(2)}) copy-start(f32[2]{0:T(128)S(1)} %get-tuple-element.54) | copy-start | bytes 28
  334.5 68.6 %copy-start.186 = (f32[2]{0:T(128)}, f32[2]{0:T(128)S(1)}, u32[]{:S(2)}) copy-start(f32[2]{0:T(128)S(1)} %get-tuple-element.53) | copy-start | bytes 28
  352.1 36.3 %copy-start.6 = (f32[1,1024,128]{2,1,0:T(8,128)}, f32[1,1024,128]{2,1,0:T(8,128)S(1)}, u32[]{:S(2)}) copy-start(f32[1,1024,128]{2,1,0:T(8,128)S(1)} %get-tuple-element.146) | copy-start | bytes 1572868
  352.3 36.1 %copy-start.132 = (f32[4,2]{1,0:T(4,128)}, f32[4,2]{1,0:T(4,128)S(1)}, u32[]{:S(2)}) copy-start(f32[4,2]{1,0:T(4,128)S(1)} %copy.275) | copy-start | bytes 100
  352.4 48.6 %copy-start.107 = (f32[4,256,2]{1,2,0:T(2,128)}, f32[4,256,2]{1,2,0:T(2,128)S(1)}, u32[]{:S(2)}) copy-start(f32[4,256,2]{1,2,0:T(2,128)S(1)} %multiply_bitcast_fusion.6) | copy-start | bytes 24580
  540.9 52.3 %copy-start.78 = (f32[1,1,2,128,64]{3,4,2,1,0:T(8,128)S(1)}, f32[1,1,2,128,64]{3,4,2,1,0:T(8,128)}, u32[]{:S(2)}) copy-start(f32[1,1,2,128,64]{3,4,2,1,0:T(8,128)} %copy-done.77) | copy-start | bytes 196612
  541.7 52.8 %copy-start.76 = (f32[1,1,2,128,64]{3,4,2,1,0:T(8,128)S(1)}, f32[1,1,2,128,64]{3,4,2,1,0:T(8,128)}, u32[]{:S(2)}) copy-start(f32[1,1,2,128,64]{3,4,2,1,0:T(8,128)} %copy-done.75) | copy-start | bytes 196612
  541.8 55.4 %copy-start.8 = (f32[1,1024,128]{2,1,0:T(8,128)S(1)}, f32[1,1024,128]{2,1,0:T(8,128)}, u32[]{:S(2)}) copy-start(f32[1,1024,128]{2,1,0:T(8,128)} %copy-done.6) | copy-start | bytes 1572868
  542.6 91.9 %reduce-scatter.15.cloned.1.call-start = ((), (), s32[]{:S(2)}) async-start(), calls=%async_computation.14 | async-start | bytes 1310720 | tf_op jit(solution)/shard_map/reduce_scatter | solution.py:258
  608.6 141.4 %reduce-scatter.13.cloned.1.call-start = ((), (), s32[]{:S(2)}) async-start(), calls=%async_computation.10 | async-start | bytes 4456448 | tf_op jit(solution)/shard_map/reduce_scatter | solution.py:189
  611.9 138.2 %all-gather.19.cloned.1.call-start = ((), (), s32[]{:S(2)}) async-start(), calls=%async_computation.15 | async-start | bytes 1310720 | tf_op jit(solution)/shard_map/all_gather | solution.py:266
  634.5 141.9 %all-gather.13.cloned.1.call-start = ((), (), s32[]{:S(2)}) async-start(), calls=%async_computation.11 | async-start | bytes 1310720 | tf_op jit(solution)/shard_map/all_gather | solution.py:195
  750.0 64.3 %all-gather.21.cloned.1.call-start = ((), (), s32[]{:S(2)}) async-start(), calls=%async_computation.16 | async-start | bytes 2621440 | tf_op jit(solution)/shard_map/all_gather | solution.py:207
  779.7 176.1 %all-gather.23.cloned.1.call-start = ((), (), s32[]{:S(2)}) async-start(), calls=%async_computation.17 | async-start | bytes 2621440 | tf_op jit(solution)/shard_map/all_gather | solution.py:231
  893.7 51.3 %copy-start.24 = (f32[1,4,256,2,64]{2,4,3,1,0:T(8,128)S(1)}, f32[1,4,256,2,64]{2,4,3,1,0:T(8,128)}, u32[]{:S(2)}) copy-start(f32[1,4,256,2,64]{2,4,3,1,0:T(8,128)} %copy-done.23) | copy-start | bytes 1572868
  894.6 90.5 %reduce-scatter.17.cloned.1.call-start = ((), (), s32[]{:S(2)}) async-start(), calls=%async_computation.18 | async-start | bytes 1310720 | tf_op jit(solution)/shard_map/reduce_scatter | solution.py:258
  959.9 53.4 %all-gather.25.cloned.1.call-start = ((), (), s32[]{:S(2)}) async-start(), calls=%async_computation.19 | async-start | bytes 1310720 | tf_op jit(solution)/shard_map/all_gather | solution.py:266
  985.2 37.4 %all-reduce.84.cloned.1.call-start = ((), (), s32[]{:S(2)}) async-start(), calls=%async_computation.21 | async-start | bytes 3145728 | tf_op jit(solution)/shard_map/psum | solution.py:108
  994.7 161.4 %all-reduce.82.cloned.1.call-start = ((), (), s32[]{:S(2)}) async-start(), calls=%async_computation.20 | async-start | bytes 4194304 | tf_op jit(solution)/shard_map/psum | solution.py:112
  1026.8 42.6 %copy-start.37 = (f32[256,1024]{1,0:T(8,128)S(1)}, f32[256,1024]{1,0:T(8,128)}, u32[]{:S(2)}) copy-start(f32[256,1024]{1,0:T(8,128)} %get-tuple-element.111) | copy-start | bytes 3145732
  1026.8 42.6 %copy-start.192 = (f32[256]{0:T(256)S(1)}, f32[256]{0:T(256)}, u32[]{:S(2)}) copy-start(f32[256]{0:T(256)} %get-tuple-element.214) | copy-start | bytes 3076
  (187 other events, 996.1 us)
Sparse Core Ops, SparseCore 0:
  26.5 77.8 reduce-scatter.6
  170.0 93.7 reduce-scatter.8
  265.4 26.4 all-gather.10
  309.5 76.5 reduce-scatter.10
  542.8 43.7 all-gather.16
  634.7 45.0 all-gather.18
  750.2 26.2 all-gather.12
  894.7 43.2 all-gather.22
  985.3 27.9 all-gather.24
Sparse Core Ops, SparseCore 1:
  311.8 36.3 all-gather.14
  608.7 25.8 reduce-scatter.14
  636.7 113.3 reduce-scatter.12
  779.8 34.4 all-gather.20
  960.0 25.1 reduce-scatter.16
  994.7 20.0 all-reduce.83
  1022.0 134.0 all-reduce.81
where the time goes:
time: 1180 us; the launch traced here: 1170 us
  waiting for transfers between devices  476 us (40%)
  blocking collectives  320 us (27%)
  other arithmetic  141 us (12%)
  matrix products  104 us (9%)
  local copies, waits for them, and re-layouts  102 us (9%)
  between operations  21.9 us (2%)
    reduce_scatter x2, waiting for transfers between devices, shards(): lax.psum_scatter(project(jnp.int32(0), lax.axis_size(('row', 'col')) * ke...  209 us
    psum x1, waiting for transfers between devices, total_shared(): return lax.psum(terms, ('dp', 'row', 'col'))  85.3 us
    psum x2, blocking collectives, shards(): squares = lax.psum(jnp.sum(gated * gated, axis=1), ('row', 'col'))  83.3 us
    psum x2, blocking collectives, shards(): inner_dot = lax.psum(jnp.sum(gated * weighted, axis=1), ('row', 'col'))  78.5 us
    reduce_scatter x2, waiting for transfers between devices, shards(): lax.psum_scatter(part_mixed, 'col', scatter_dimension=1, tiled=True)  51.9 us
    all_gather x2, waiting for transfers between devices, shards(): branch = lax.all_gather(shared_rows, 'col', axis=0, tiled=True)  46 us
    reduce_scatter x2, waiting for transfers between devices, shards(): lax.psum_scatter(back_rows(jnp.int32(0), lax.axis_size('row') * (mixed_ro...  41 us
    psum x1, blocking collectives, total_shared(): return lax.psum(terms, ('dp', 'row', 'col'))  40.7 us
  transfers between devices with their start and end apart: 16, of which 11 were waited for; matrix products, arithmetic and copies ran while one was open for 17% of the time, Pallas kernels for 0%

commit v1 on v0

--- a/solution.py
+++ b/solution.py
@@ -204,7 +204,15 @@
             layer_index
         ]
         grad_low = grad.astype(jnp.bfloat16)
-        grad_full = lax.all_gather(grad_low, "row", axis=0, tiled=True)
+        ways, here = (lax.axis_size("row"), lax.axis_index("row"))
+        grown, reach = (grad_low, 1)
+        while reach < ways:
+            theirs = lax.ppermute(grown, "row", [(d, d ^ reach) for d in range(ways)])
+            mine_first = jnp.concatenate([grown, theirs], axis=0)
+            theirs_first = jnp.concatenate([theirs, grown], axis=0)
+            grown = jnp.where(here & reach == 0, mine_first, theirs_first)
+            reach = 2 * reach
+        grad_full = grown
         grad_out_w = lax.dot_general(
             normed_out, grad_full, CONTRACT_ROWS, preferred_element_type=jnp.float32
         )

time: 1180 us -> 1220 us (1.034)
  waiting for transfers between devices: 476 us -> 511 us
    ppermute x0 -> x4, waiting for transfers between devices: none -> 42.4 us  [shards(): theirs = lax.ppermute(grown, 'row', [(d, d ^ reach) for d in range(ways)])]
    all_gather x2 -> x0, waiting for transfers between devices: 30.7 us -> none  [shards(): grad_full = lax.all_gather(grad_low, 'row', axis=0, tiled=True)]
    all_gather x2, waiting for transfers between devices: 10.6 us -> 39.5 us  [shards(): lax.all_gather(summed.astype(jnp.bfloat16), 'col', axis=1, tiled=True)]
    reduce_scatter x2, waiting for transfers between devices: 209 us -> 193 us  [shards(): lax.psum_scatter(project(jnp.int32(0), lax.axis_size(('row', 'col')) * ke...]
    psum x1, waiting for transfers between devices: 0.02 us -> 14 us  [total_heads(): lax.psum(shortened(terms), 'dp')]
  transfers between devices with their start and end apart: 16 -> 18, of which waited for: 11 -> 15; matrix products, arithmetic and copies ran while one was open for 17% -> 17% of each run, Pallas kernels for 0% -> 0%
where the time goes in v1:
time: 1220 us; the launch traced here: 1210 us
  waiting for transfers between devices  511 us (42%)
  blocking collectives  317 us (26%)
  other arithmetic  145 us (12%)
  matrix products  107 us (9%)
  local copies, waits for them, and re-layouts  100 us (8%)
  between operations  20.5 us (2%)
    reduce_scatter x2, waiting for transfers between devices, shards(): lax.psum_scatter(project(jnp.int32(0), lax.axis_size(('row', 'col')) * ke...  193 us
    psum x1, waiting for transfers between devices, total_shared(): return lax.psum(terms, ('dp', 'row', 'col'))  93.2 us
    psum x2, blocking collectives, shards(): squares = lax.psum(jnp.sum(gated * gated, axis=1), ('row', 'col'))  83.3 us
    psum x2, blocking collectives, shards(): inner_dot = lax.psum(jnp.sum(gated * weighted, axis=1), ('row', 'col'))  79.4 us
    all_gather x2, waiting for transfers between devices, shards(): branch = lax.all_gather(shared_rows, 'col', axis=0, tiled=True)  48.9 us
    ppermute x4, waiting for transfers between devices, shards(): theirs = lax.ppermute(grown, 'row', [(d, d ^ reach) for d in range(ways)])  42.4 us
    reduce_scatter x2, waiting for transfers between devices, shards(): lax.psum_scatter(part_mixed, 'col', scatter_dimension=1, tiled=True)  41.6 us
    psum x1, blocking collectives, total_shared(): return lax.psum(terms, ('dp', 'row', 'col'))  41.4 us
  transfers between devices with their start and end apart: 18, of which 15 were waited for; matrix products, arithmetic and copies ran while one was open for 17% of the time, Pallas kernels for 0%

profile of v1, /device:TPU:0, one launch (start us, length us, event | category | flops | bytes accessed | tf_op | source)
XLA Modules:
  0.0 1208.5 jit_solution(473634511909515958)
XLA Ops:
  11.1 11.5 all_gather.36
  22.7 2.7 fusion.148
  27.5 20.9 %all-reduce.74 = bf16[1024,8]{0,1:T(8,128)(2,1)S(1)} all-reduce(f32[1024,8]{0,1:T(8,128)S(1)} %fusion.316), channel_id=5, replica_groups=mesh['dp'=2,'row'=4,'col'=4] {'col'}, use_global_device_ids=true, to_apply=%region_2.0.clone | all-reduce | flops 8192 | bytes 49152
  49.7 2.4 reduce-window.26
  60.7 9.9 all_gather.37
  81.4 22.0 %reduce-scatter.7.cloned.1.call-done = f32[1024,256]{1,0:T(8,128)} async-done(((f32[1024,1024]{1,0:T(8,128)}), f32[1024,256]{1,0:T(8,128)}) %reduce-scatter.7.cloned.1.call-update) | async-done | bytes 1048592 | tf_op jit(solution)/shard_map/reduce_scatter | solution.py:162
  105.7 2.5 copy.258
  119.2 3.7 multiply_reduce_fusion.29
  122.9 41.3 %psum.119 = f32[1024]{0:T(1024)S(1)} all-reduce(f32[1024]{0:T(1024)S(1)} %bitcast.1224), channel_id=1, replica_groups=mesh['dp'=2,'row'=4,'col'=4] {'row','col'}, use_global_device_ids=true, to_apply=%region_6.8 | all-reduce | flops 1024 | bytes 8192 | tf_op jit(solution)/shard_map/psum | solution.py:181
  166.3 2.7 fusion.186
  169.1 93.7 %reduce-scatter.9.cloned.1.call-done = f32[64,1024]{1,0:T(8,128)} async-done(((f32[1024,1024]{1,0:T(8,128)}), f32[64,1024]{1,0:T(8,128)}) %reduce-scatter.9.cloned.1.call-update) | async-done | bytes 262160 | tf_op jit(solution)/shard_map/reduce_scatter | solution.py:189
  262.9 28.2 %all-gather.9.cloned.1.call-done = f32[256,1024]{1,0:T(8,128)} async-done(((f32[64,1024]{1,0:T(8,128)}), f32[256,1024]{1,0:T(8,128)}) %all-gather.9.cloned.1.call-update) | async-done | bytes 1048592 | tf_op jit(solution)/shard_map/all_gather | solution.py:195
  294.1 10.5 all_gather.39
  304.6 3.9 fusion.142
  311.4 9.8 collective-permute-done
  321.2 2.7 maximum_select_fusion.2
  325.2 19.9 %all-reduce.75 = bf16[1024,8]{0,1:T(8,128)(2,1)S(1)} all-reduce(f32[1024,8]{0,1:T(8,128)S(1)} %fusion.313), channel_id=8, replica_groups=mesh['dp'=2,'row'=4,'col'=4] {'col'}, use_global_device_ids=true, to_apply=%region_10.12.clone | all-reduce | flops 8192 | bytes 49152
  345.4 2.4 reduce-window.30
  350.6 8.9 all_gather.40
  365.9 19.5 %reduce-scatter.11.cloned.1.call-done = f32[1024,256]{1,0:T(8,128)} async-done(((f32[1024,1024]{1,0:T(8,128)}), f32[1024,256]{1,0:T(8,128)}) %reduce-scatter.11.cloned.1.call-update) | async-done | bytes 1048592 | tf_op jit(solution)/shard_map/reduce_scatter | solution.py:162
  385.4 2.3 convert_convert_fusion
  387.7 2.5 copy.270
  406.5 3.6 multiply_reduce_fusion.28
  412.7 42.0 %psum.120 = f32[1024]{0:T(1024)} all-reduce(f32[1024]{0:T(1024)} %bitcast.1223), channel_id=1, replica_groups=mesh['dp'=2,'row'=4,'col'=4] {'row','col'}, use_global_device_ids=true, to_apply=%region_14.16 | all-reduce | flops 1024 | bytes 8192 | tf_op jit(solution)/shard_map/psum | solution.py:181
  456.0 5.3 multiply_reduce_fusion.14
  461.3 37.6 %psum.121 = f32[1024]{0:T(1024)} all-reduce(f32[1024]{0:T(1024)} %get-tuple-element.34), channel_id=1, replica_groups=mesh['dp'=2,'row'=4,'col'=4] {'row','col'}, use_global_device_ids=true, to_apply=%region_17.19 | all-reduce | flops 1024 | bytes 8192 | tf_op jit(solution)/shard_map/psum | solution.py:224
  499.6 3.1 fusion.124
  506.2 5.9 fusion.31
  518.0 2.5 convolution_bitcast_fusion.4
  528.3 3.7 fusion.36
  554.6 11.2 reduce-window.34
  578.2 14.1 %all-gather = bf16[1,1024,8]{1,0,2:T(2,128)(2,1)} all-gather(bf16[1,1024,2]{1,0,2:T(2,128)(2,1)S(1)} %copy.297), channel_id=2, replica_groups=mesh['dp'=2,'row'=4,'col'=4] {'col'}, dimensions={2}, use_global_device_ids=true | all-gather | bytes 20480 | tf_op jit(solution)/shard_map/all_gather | solution.py:240
  603.8 2.4 fusion.140
  608.2 2.7 fusion.183
  611.0 22.6 %reduce-scatter.15.cloned.1.call-done = bf16[256,512]{1,0:T(8,128)(2,1)} async-done(((bf16[1024,512]{1,0:T(8,128)(2,1)}), bf16[256,512]{1,0:T(8,128)(2,1)}) %reduce-scatter.15.cloned.1.call-update) | async-done | bytes 262160 | tf_op jit(solution)/shard_map/reduce_scatter | solution.py:266
  633.6 99.6 %reduce-scatter.13.cloned.1.call-done = f32[64,1024]{1,0:T(8,128)} async-done(((f32[1024,1024]{1,0:T(8,128)}), f32[64,1024]{1,0:T(8,128)}) %reduce-scatter.13.cloned.1.call-update) | async-done | bytes 262160 | tf_op jit(solution)/shard_map/reduce_scatter | solution.py:189
  733.3 28.2 %all-gather.15.cloned.1.call-done = bf16[256,2048]{1,0:T(8,128)(2,1)} async-done(((bf16[256,512]{1,0:T(8,128)(2,1)}), bf16[256,2048]{1,0:T(8,128)(2,1)}) %all-gather.15.cloned.1.call-update) | async-done | bytes 1048592 | tf_op jit(solution)/shard_map/all_gather | solution.py:274
  761.4 3.7 reshape.2426
  765.1 2.4 slice_reduce_fusion.1
  769.7 20.8 %all-gather.11.cloned.1.call-done = f32[256,1024]{1,0:T(8,128)} async-done(((f32[64,1024]{1,0:T(8,128)}), f32[256,1024]{1,0:T(8,128)}) %all-gather.11.cloned.1.call-update) | async-done | bytes 1048592 | tf_op jit(solution)/shard_map/all_gather | solution.py:195
  790.4 3.2 fusion.373
  795.1 11.7 collective-permute-done.2
  811.2 20.9 %collective-permute-done.3 = bf16[512,1024]{1,0:T(8,128)(2,1)} collective-permute-done((bf16[512,1024]{1,0:T(8,128)(2,1)}, bf16[512,1024]{1,0:T(8,128)(2,1)}, u32[]{:S(2)}, u32[]{:S(2)}) %collective-permute-start.3) | collective-permute-done | bytes 1048608 | tf_op jit(solution)/shard_map/ppermute | solution.py:210
  832.1 5.1 multiply_reduce_fusion.15
  837.2 41.8 %psum.122 = f32[1024]{0:T(1024)S(1)} all-reduce(f32[1024]{0:T(1024)S(1)} %get-tuple-element.32), channel_id=1, replica_groups=mesh['dp'=2,'row'=4,'col'=4] {'row','col'}, use_global_device_ids=true, to_apply=%region_35.37 | all-reduce | flops 1024 | bytes 8192 | tf_op jit(solution)/shard_map/psum | solution.py:224
  879.0 3.2 fusion.125
  885.8 5.5 fusion.33
  900.4 3.7 fusion.45
  926.8 11.3 reduce-window.36
  950.4 13.9 %all-gather.1 = bf16[1,1024,8]{1,0,2:T(2,128)(2,1)} all-gather(bf16[1,1024,2]{1,0,2:T(2,128)(2,1)S(1)} %copy.319), channel_id=3, replica_groups=mesh['dp'=2,'row'=4,'col'=4] {'col'}, dimensions={2}, use_global_device_ids=true | all-gather | bytes 20480 | tf_op jit(solution)/shard_map/all_gather | solution.py:240
  967.9 2.3 fusion.35
  975.3 2.4 fusion.146
  982.0 3.1 fusion.55
  988.0 15.9 %reduce-scatter.17.cloned.1.call-done = bf16[256,512]{1,0:T(8,128)(2,1)} async-done(((bf16[1024,512]{1,0:T(8,128)(2,1)}), bf16[256,512]{1,0:T(8,128)(2,1)}) %reduce-scatter.17.cloned.1.call-update) | async-done | bytes 262160 | tf_op jit(solution)/shard_map/reduce_scatter | solution.py:266
  1008.1 3.1 fusion.54
  1014.4 3.6 all-reduce.77
  1022.1 11.3 all-gather.19.cloned.1.call-done
  1033.4 3.7 reshape.2428
  1037.1 2.3 slice_reduce_fusion
  1042.7 14.0 %all-reduce.84.cloned.1.call-done = (bf16[2,256,1024]{2,1,0:T(8,128)(2,1)}, bf16[2,128,1024]{2,1,0:T(8,128)(2,1)}) async-done(((bf16[2,256,1024]{2,1,0:T(8,128)(2,1)}, bf16[2,128,1024]{2,1,0:T(8,128)(2,1)}), (bf16[2,256,1024]{2,1,0:T(8,128)(2,1)}, bf16[2,128,1024]{2,1,0:T(8,128)(2,1)})) %all-reduce.84.cloned.1.call-update) | async-done | bytes 1572880 | tf_op jit(solution)/shard_map/psum | solution.py:108
  1056.7 2.8 convert_element_type.209
  1062.7 41.4 %all-reduce.76 = (f32[2,1024]{1,0:T(2,128)}, f32[2,4,256]{2,1,0:T(4,128)}, f32[2,256]{1,0:T(2,128)}) all-reduce(f32[2,1024]{1,0:T(2,128)S(1)} %pad_maximum_fusion.5, f32[2,4,256]{2,1,0:T(4,128)S(1)} %pad_maximum_fusion.7, f32[2,256]{1,0:T(2,128)S(1)} %pad_maximum_fusion.9), channel_id=1, replica_groups=mesh['dp'=2,'row'=4,'col'=4] {'dp','row','col'}, use_global_device_ids=true, to_apply=%region_54.56 | all-reduce | flops 4608 | bytes 36864 | tf_op jit(solution)/shard_map/psum | solution.py:112
  1105.5 93.2 %all-reduce.82.cloned.1.call-done = f32[2,1024,256]{2,1,0:T(8,128)} async-done(((f32[2,1024,256]{2,1,0:T(8,128)}), f32[2,1024,256]{2,1,0:T(8,128)}) %all-reduce.82.cloned.1.call-update) | async-done | bytes 2097168 | tf_op jit(solution)/shard_map/psum | solution.py:112
  1198.7 3.0 copy.438
  (805 shorter events, 230.4 us)
Async XLA Ops:
  7.2 96.3 %reduce-scatter.7.cloned.1.call-start = ((), (), s32[]{:S(2)}) async-start(), calls=%async_computation.6 | async-start | bytes 5242880 | tf_op jit(solution)/shard_map/reduce_scatter | solution.py:162
  8.1 285.1 %copy-start.117 = (f32[1,1024]{1,0:T(1,128)}, f32[1,1024]{1,0:T(1,128)S(1)}, u32[]{:S(2)}) copy-start(f32[1,1024]{1,0:T(1,128)S(1)} %get-tuple-element.187) | copy-start | bytes 12292
  11.1 49.3 %copy-start.56 = (bf16[256,1024]{1,0:T(8,128)(2,1)}, bf16[256,1024]{1,0:T(8,128)(2,1)S(1)}, u32[]{:S(2)}) copy-start(bf16[256,1024]{1,0:T(8,128)(2,1)S(1)} %fusion.68) | copy-start | bytes 1572868
  25.5 45.5 %copy-start.227 = (f32[2,128]{1,0:T(2,128)S(1)}, f32[2,128]{1,0:T(2,128)}, u32[]{:S(2)}) copy-start(f32[2,128]{1,0:T(2,128)} %param.25) | copy-start | bytes 3076
  25.5 46.1 %copy-start.228 = (f32[2,2]{1,0:T(2,128)S(1)}, f32[2,2]{1,0:T(2,128)}, u32[]{:S(2)}) copy-start(f32[2,2]{1,0:T(2,128)} %param.30) | copy-start | bytes 52
  25.5 46.6 %copy-start.221 = (f32[2,256]{1,0:T(2,128)S(1)}, f32[2,256]{1,0:T(2,128)}, u32[]{:S(2)}) copy-start(f32[2,256]{1,0:T(2,128)} %param.27) | copy-start | bytes 6148
  25.5 47.1 %copy-start.207 = (f32[2,4,128]{2,1,0:T(4,128)S(1)}, f32[2,4,128]{2,1,0:T(4,128)}, u32[]{:S(2)}) copy-start(f32[2,4,128]{2,1,0:T(4,128)} %param.24) | copy-start | bytes 12292
  25.5 49.8 %copy-start.173 = (f32[2,4,256]{2,1,0:T(4,128)S(1)}, f32[2,4,256]{2,1,0:T(4,128)}, u32[]{:S(2)}) copy-start(f32[2,4,256]{2,1,0:T(4,128)} %param.26) | copy-start | bytes 24580
  25.5 237.3 %reduce-scatter.9.cloned.1.call-start = ((), (), s32[]{:S(2)}) async-start(), calls=%async_computation.7 | async-start | bytes 4456448 | tf_op jit(solution)/shard_map/reduce_scatter | solution.py:189
  49.6 69.5 %copy-start.101 = (f32[1,1024,2]{1,2,0:T(2,128)}, f32[1,1024,2]{1,2,0:T(2,128)S(1)}, u32[]{:S(2)}) copy-start(f32[1,1024,2]{1,2,0:T(2,128)S(1)} %compare_select_fusion.5) | copy-start | bytes 24580
  70.9 47.1 %copy-start.166 = (f32[2]{0:T(128)}, f32[2]{0:T(128)S(1)}, u32[]{:S(2)}) copy-start(f32[2]{0:T(128)S(1)} %get-tuple-element.56) | copy-start | bytes 28
  70.9 47.1 %copy-start.190 = (f32[2]{0:T(128)}, f32[2]{0:T(128)S(1)}, u32[]{:S(2)}) copy-start(f32[2]{0:T(128)S(1)} %get-tuple-element.55) | copy-start | bytes 28
  73.2 37.2 %copy-start.174 = (f32[128]{0:T(128)}, f32[128]{0:T(128)S(1)}, u32[]{:S(2)}) copy-start(f32[128]{0:T(128)S(1)} %get-tuple-element.201) | copy-start | bytes 1540
  73.2 37.2 %copy-start.176 = (f32[128]{0:T(128)}, f32[128]{0:T(128)S(1)}, u32[]{:S(2)}) copy-start(f32[128]{0:T(128)S(1)} %get-tuple-element.198) | copy-start | bytes 1540
  73.2 37.2 %copy-start.178 = (f32[128]{0:T(128)}, f32[128]{0:T(128)S(1)}, u32[]{:S(2)}) copy-start(f32[128]{0:T(128)S(1)} %get-tuple-element.199) | copy-start | bytes 1540
  73.2 37.2 %copy-start.180 = (f32[128]{0:T(128)}, f32[128]{0:T(128)S(1)}, u32[]{:S(2)}) copy-start(f32[128]{0:T(128)S(1)} %get-tuple-element.200) | copy-start | bytes 1540
  75.3 285.1 %copy-start.105 = (f32[4,256]{1,0:T(4,128)}, f32[4,256]{1,0:T(4,128)S(1)}, u32[]{:S(2)}) copy-start(f32[4,256]{1,0:T(4,128)S(1)} %compare_convert_fusion.6) | copy-start | bytes 12292
  75.3 43.8 %copy-start.129 = (f32[256,2]{0,1:T(2,128)}, f32[256,2]{0,1:T(2,128)S(1)}, u32[]{:S(2)}) copy-start(f32[256,2]{0,1:T(2,128)S(1)} %get-tuple-element.189) | copy-start | bytes 6148
  75.3 43.8 %copy-start.131 = (f32[256,2]{0,1:T(2,128)}, f32[256,2]{0,1:T(2,128)S(1)}, u32[]{:S(2)}) copy-start(f32[256,2]{0,1:T(2,128)S(1)} %get-tuple-element.190) | copy-start | bytes 6148
  75.3 43.8 %copy-start.133 = (f32[256,2]{0,1:T(2,128)}, f32[256,2]{0,1:T(2,128)S(1)}, u32[]{:S(2)}) copy-start(f32[256,2]{0,1:T(2,128)S(1)} %get-tuple-element.191) | copy-start | bytes 6148
  76.0 316.3 %copy-start.89 = (f32[1,1024]{1,0:T(1,128)}, f32[1,1024]{1,0:T(1,128)S(1)}, u32[]{:S(2)}) copy-start(f32[1,1024]{1,0:T(1,128)S(1)} %get-tuple-element.207) | copy-start | bytes 12292
  76.0 316.3 %copy-start.92 = (f32[1,1024]{1,0:T(1,128)}, f32[1,1024]{1,0:T(1,128)S(1)}, u32[]{:S(2)}) copy-start(f32[1,1024]{1,0:T(1,128)S(1)} %get-tuple-element.208) | copy-start | bytes 12292
  76.1 316.3 %copy-start.95 = (f32[1,1024]{1,0:T(1,128)}, f32[1,1024]{1,0:T(1,128)S(1)}, u32[]{:S(2)}) copy-start(f32[1,1024]{1,0:T(1,128)S(1)} %get-tuple-element.209) | copy-start | bytes 12292
  76.2 41.1 %copy-start.111 = (f32[4,256,2]{1,2,0:T(2,128)}, f32[4,256,2]{1,2,0:T(2,128)S(1)}, u32[]{:S(2)}) copy-start(f32[4,256,2]{1,2,0:T(2,128)S(1)} %multiply_bitcast_fusion.7) | copy-start | bytes 24580
  79.5 37.8 %copy-start.4 = (f32[1,1024,128]{2,1,0:T(8,128)}, f32[1,1024,128]{2,1,0:T(8,128)S(1)}, u32[]{:S(2)}) copy-start(f32[1,1024,128]{2,1,0:T(8,128)S(1)} %get-tuple-element.150) | copy-start | bytes 1572868
  79.5 39.3 %copy-start.13 = (f32[1,1024,128]{2,1,0:T(8,128)}, f32[1,1024,128]{2,1,0:T(8,128)S(1)}, u32[]{:S(2)}) copy-start(f32[1,1024,128]{2,1,0:T(8,128)S(1)} %get-tuple-element.151) | copy-start | bytes 1572868
  119.2 45.6 %copy-start.224 = (f32[2,64]{1,0:T(2,128)S(1)}, f32[2,64]{1,0:T(2,128)}, u32[]{:S(2)}) copy-start(f32[2,64]{1,0:T(2,128)} %mul.2202) | copy-start | bytes 1540
  119.2 47.0 %copy-start.81 = (bf16[2,128,1024]{2,1,0:T(8,128)(2,1)S(1)}, bf16[2,128,1024]{2,1,0:T(8,128)(2,1)}, u32[]{:S(2)}) copy-start(bf16[2,128,1024]{2,1,0:T(8,128)(2,1)} %param.32) | copy-start | bytes 1572868
  169.0 122.1 %copy-start.2 = (bf16[256,1024]{1,0:T(8,128)(2,1)S(1)}, bf16[256,1024]{1,0:T(8,128)(2,1)}, u32[]{:S(2)}) copy-start(bf16[256,1024]{1,0:T(8,128)(2,1)} %param.17) | copy-start | bytes 1572868
  169.0 122.0 %all-gather.9.cloned.1.call-start = ((), (), s32[]{:S(2)}) async-start(), calls=%async_computation.8 | async-start | bytes 1310720 | tf_op jit(solution)/shard_map/all_gather | solution.py:195
  262.8 122.6 %reduce-scatter.11.cloned.1.call-start = ((), (), s32[]{:S(2)}) async-start(), calls=%async_computation.9 | async-start | bytes 5242880 | tf_op jit(solution)/shard_map/reduce_scatter | solution.py:162
  308.5 36.7 %copy-start.197 = (f32[2]{0:T(128)S(1)}, f32[2]{0:T(128)}, u32[]{:S(2)}) copy-start(f32[2]{0:T(128)} %get-tuple-element.228) | copy-start | bytes 28
  308.6 36.8 %copy-start.195 = (f32[2]{0:T(128)S(1)}, f32[2]{0:T(128)}, u32[]{:S(2)}) copy-start(f32[2]{0:T(128)} %get-tuple-element.226) | copy-start | bytes 28
  308.6 40.7 %copy-start.62 = (bf16[256,1024]{1,0:T(8,128)(2,1)S(1)}, bf16[256,1024]{1,0:T(8,128)(2,1)}, u32[]{:S(2)}) copy-start(bf16[256,1024]{1,0:T(8,128)(2,1)} %copy-done.61) | copy-start | bytes 1572868
  308.6 295.0 %all-gather.13.cloned.1.call-start = ((), (), s32[]{:S(2)}) async-start(), calls=%async_computation.12 | async-start | bytes 2621440 | tf_op jit(solution)/shard_map/all_gather | solution.py:239
  309.6 11.7 collective-permute-start
  311.4 48.3 %copy-start.141 = (f32[1,1,256]{2,1,0:T(1,128)S(1)}, f32[1,1,256]{2,1,0:T(1,128)}, u32[]{:S(2)}) copy-start(f32[1,1,256]{2,1,0:T(1,128)} %copy-done.140) | copy-start | bytes 3076
  311.4 48.3 %copy-start.143 = (f32[1,1,256]{2,1,0:T(1,128)S(1)}, f32[1,1,256]{2,1,0:T(1,128)}, u32[]{:S(2)}) copy-start(f32[1,1,256]{2,1,0:T(1,128)} %copy-done.142) | copy-start | bytes 3076
  311.4 48.3 %copy-start.145 = (f32[1,1,256]{2,1,0:T(1,128)S(1)}, f32[1,1,256]{2,1,0:T(1,128)}, u32[]{:S(2)}) copy-start(f32[1,1,256]{2,1,0:T(1,128)} %copy-done.144) | copy-start | bytes 3076
  323.9 132.1 %collective-permute-start.1 = (bf16[512,1024]{1,0:T(8,128)(2,1)}, bf16[512,1024]{1,0:T(8,128)(2,1)}, u32[]{:S(2)}, u32[]{:S(2)}) collective-permute-start(bf16[512,1024]{1,0:T(8,128)(2,1)} %maximum_select_fusion.2), channel_id=1, source_target_pairs={{0,8},{4,12},{8,0},{12,4},{1,9},{5,13},{9,1},{13,5},{2,10},{6,14},... | collective-permute-start | bytes 3145736 | tf_op jit(solution)/shard_map/ppermute | solution.py:210
  325.2 35.4 %copy-start.158 = (f32[1,1,256]{2,1,0:T(1,128)S(1)}, f32[1,1,256]{2,1,0:T(1,128)}, u32[]{:S(2)}) copy-start(f32[1,1,256]{2,1,0:T(1,128)} %get-tuple-element.186) | copy-start | bytes 3076
  325.2 35.4 %copy-start.160 = (f32[1,1,256]{2,1,0:T(1,128)S(1)}, f32[1,1,256]{2,1,0:T(1,128)}, u32[]{:S(2)}) copy-start(f32[1,1,256]{2,1,0:T(1,128)} %get-tuple-element.180) | copy-start | bytes 3076
  325.2 35.4 %copy-start.164 = (f32[1,1,256]{2,1,0:T(1,128)S(1)}, f32[1,1,256]{2,1,0:T(1,128)}, u32[]{:S(2)}) copy-start(f32[1,1,256]{2,1,0:T(1,128)} %get-tuple-element.179) | copy-start | bytes 3076
  325.2 35.4 %copy-start.199 = (f32[1,256]{1,0:T(1,128)S(1)}, f32[1,256]{1,0:T(1,128)}, u32[]{:S(2)}) copy-start(f32[1,256]{1,0:T(1,128)} %get-tuple-element.210) | copy-start | bytes 3076
  359.8 42.6 %copy-start.168 = (f32[2]{0:T(128)}, f32[2]{0:T(128)S(1)}, u32[]{:S(2)}) copy-start(f32[2]{0:T(128)S(1)} %get-tuple-element.54) | copy-start | bytes 28
  359.8 42.6 %copy-start.192 = (f32[2]{0:T(128)}, f32[2]{0:T(128)S(1)}, u32[]{:S(2)}) copy-start(f32[2]{0:T(128)S(1)} %get-tuple-element.53) | copy-start | bytes 28
  360.5 39.8 %copy-start.113 = (f32[4,256,2]{1,2,0:T(2,128)}, f32[4,256,2]{1,2,0:T(2,128)S(1)}, u32[]{:S(2)}) copy-start(f32[4,256,2]{1,2,0:T(2,128)S(1)} %multiply_bitcast_fusion.6) | copy-start | bytes 24580
  540.3 52.0 %copy-start.80 = (f32[1,1,2,128,64]{3,4,2,1,0:T(8,128)S(1)}, f32[1,1,2,128,64]{3,4,2,1,0:T(8,128)}, u32[]{:S(2)}) copy-start(f32[1,1,2,128,64]{3,4,2,1,0:T(8,128)} %copy-done.79) | copy-start | bytes 196612
  541.1 52.6 %copy-start.78 = (f32[1,1,2,128,64]{3,4,2,1,0:T(8,128)S(1)}, f32[1,1,2,128,64]{3,4,2,1,0:T(8,128)}, u32[]{:S(2)}) copy-start(f32[1,1,2,128,64]{3,4,2,1,0:T(8,128)} %copy-done.77) | copy-start | bytes 196612
  541.1 55.2 %copy-start.8 = (f32[1,1024,128]{2,1,0:T(8,128)S(1)}, f32[1,1024,128]{2,1,0:T(8,128)}, u32[]{:S(2)}) copy-start(f32[1,1024,128]{2,1,0:T(8,128)} %copy-done.6) | copy-start | bytes 1572868
  542.0 91.6 %reduce-scatter.15.cloned.1.call-start = ((), (), s32[]{:S(2)}) async-start(), calls=%async_computation.13 | async-start | bytes 1310720 | tf_op jit(solution)/shard_map/reduce_scatter | solution.py:266
  607.7 125.5 %reduce-scatter.13.cloned.1.call-start = ((), (), s32[]{:S(2)}) async-start(), calls=%async_computation.10 | async-start | bytes 4456448 | tf_op jit(solution)/shard_map/reduce_scatter | solution.py:189
  611.0 150.5 %all-gather.15.cloned.1.call-start = ((), (), s32[]{:S(2)}) async-start(), calls=%async_computation.14 | async-start | bytes 1310720 | tf_op jit(solution)/shard_map/all_gather | solution.py:274
  633.6 156.8 %all-gather.11.cloned.1.call-start = ((), (), s32[]{:S(2)}) async-start(), calls=%async_computation.11 | async-start | bytes 1310720 | tf_op jit(solution)/shard_map/all_gather | solution.py:195
  733.2 242.0 %all-gather.17.cloned.1.call-start = ((), (), s32[]{:S(2)}) async-start(), calls=%async_computation.15 | async-start | bytes 2621440 | tf_op jit(solution)/shard_map/all_gather | solution.py:239
  793.6 13.2 %collective-permute-start.2 = (bf16[256,1024]{1,0:T(8,128)(2,1)S(1)}, bf16[256,1024]{1,0:T(8,128)(2,1)S(1)}, u32[]{:S(2)}, u32[]{:S(2)}) collective-permute-start(bf16[256,1024]{1,0:T(8,128)(2,1)S(1)} %get-tuple-element.110), channel_id=1, source_target_pairs={{0,4},{4,0},{8,12},{12,8},{1,5},{5,1},{9,13},{13,9},{2,6},{6,2},{1... | collective-permute-start | bytes 1572872 | tf_op jit(solution)/shard_map/ppermute | solution.py:210
  808.2 23.9 %collective-permute-start.3 = (bf16[512,1024]{1,0:T(8,128)(2,1)}, bf16[512,1024]{1,0:T(8,128)(2,1)}, u32[]{:S(2)}, u32[]{:S(2)}) collective-permute-start(bf16[512,1024]{1,0:T(8,128)(2,1)} %maximum_select_fusion.3), channel_id=1, source_target_pairs={{0,8},{4,12},{8,0},{12,4},{1,9},{5,13},{9,1},{13,5},{2,10},{6,14},... | collective-permute-start | bytes 3145736 | tf_op jit(solution)/shard_map/ppermute | solution.py:210
  913.2 51.1 %copy-start.25 = (f32[1,4,256,2,64]{2,4,3,1,0:T(8,128)S(1)}, f32[1,4,256,2,64]{2,4,3,1,0:T(8,128)}, u32[]{:S(2)}) copy-start(f32[1,4,256,2,64]{2,4,3,1,0:T(8,128)} %copy-done.24) | copy-start | bytes 1572868
  914.1 89.8 %reduce-scatter.17.cloned.1.call-start = ((), (), s32[]{:S(2)}) async-start(), calls=%async_computation.16 | async-start | bytes 1310720 | tf_op jit(solution)/shard_map/reduce_scatter | solution.py:266
  979.3 54.1 %all-gather.19.cloned.1.call-start = ((), (), s32[]{:S(2)}) async-start(), calls=%async_computation.17 | async-start | bytes 1310720 | tf_op jit(solution)/shard_map/all_gather | solution.py:274
  1003.9 52.8 %all-reduce.84.cloned.1.call-start = ((), (), s32[]{:S(2)}) async-start(), calls=%async_computation.19 | async-start | bytes 3145728 | tf_op jit(solution)/shard_map/psum | solution.py:108
  1014.0 184.6 %all-reduce.82.cloned.1.call-start = ((), (), s32[]{:S(2)}) async-start(), calls=%async_computation.18 | async-start | bytes 4194304 | tf_op jit(solution)/shard_map/psum | solution.py:112
  1060.8 43.3 %copy-start.38 = (f32[256,1024]{1,0:T(8,128)S(1)}, f32[256,1024]{1,0:T(8,128)}, u32[]{:S(2)}) copy-start(f32[256,1024]{1,0:T(8,128)} %get-tuple-element.111) | copy-start | bytes 3145732
  1060.9 43.3 %copy-start.198 = (f32[256]{0:T(256)S(1)}, f32[256]{0:T(256)}, u32[]{:S(2)}) copy-start(f32[256]{0:T(256)} %get-tuple-element.214) | copy-start | bytes 3076
  (196 other events, 1133.0 us)
Sparse Core Ops, SparseCore 0:
  25.6 77.8 reduce-scatter.6
  169.1 93.6 reduce-scatter.8
  264.4 26.6 all-gather.8
  308.7 76.6 reduce-scatter.10
  542.1 43.7 all-gather.12
  607.8 25.7 reduce-scatter.14
  635.9 97.3 reduce-scatter.12
  734.8 26.6 all-gather.14
  763.0 27.3 all-gather.10
  914.2 42.2 all-gather.16
  979.4 24.3 reduce-scatter.16
  1005.3 28.0 all-gather.18
  1036.9 19.7 all-reduce.83
  1062.5 136.1 all-reduce.81
